TPU v7x, 32 devices: a whole 2x2x4 slice. The times are simulated.
32 devices in a mesh: section: 4 (over y, x), expert: 8 (over z, core).
Axes of the slice: x: 2, y: 2, z: 4, core: 2. Of those that a mesh axis runs over, the one named last changes fastest.
Arguments:
- forward_input: bfloat16 [4, 576, 4096], P('section', 'expert'), may hold values from -6 to 6
- backward_cotangent: bfloat16 [4, 576, 4096], P('section', 'expert'), may hold values from -6 to 6
- saved_input: bfloat16 [4, 576, 4096], P('section', 'expert'), may hold values from -6 to 6
- saved_hidden: bfloat16 [4, 8, 360, 1536], P('section', 'expert'), may hold values from -8 to 8
- norm_gain: float32 [4, 4096], P('section'), may hold values from 0.5 to 2
- forward_experts: int32 [4, 576, 4], P('section', 'expert'), may hold values from 0 to 7, all different within a row; in each aligned block of 72 rows (0 to 71, 72 to 143, ..., all dimensions but the last counted through in order) at most 45 rows name the same one
- forward_gates: float32 [4, 576, 4], P('section', 'expert'), may hold values from 0.05 to 1
- backward_experts: int32 [4, 576, 4], P('section', 'expert'), may hold values from 0 to 7, all different within a row; in each aligned block of 72 rows (0 to 71, 72 to 143, ..., all dimensions but the last counted through in order) at most 45 rows name the same one
- backward_gates: float32 [4, 576, 4], P('section', 'expert'), may hold values from 0.05 to 1
- gate_up_weight: bfloat16 [4, 8, 4096, 1536], P('section', 'expert'), may hold values from -0.09375 to 0.09375
- down_weight: bfloat16 [4, 8, 768, 4096], P('section', 'expert'), may hold values from -0.21875 to 0.21875
Outputs:
- forward_output: bfloat16 [4, 576, 4096], P('section', 'expert')
- input_gradient: bfloat16 [4, 576, 4096], P('section', 'expert')
Inputs may be any that keep to these rules, and one draw needn't show every extreme that they name: `forward_experts`: each token names 4 distinct experts. In the rows of one device (aligned blocks of 72 tokens) no expert is named by more than 45 entries, and in some device's rows some expert is named by exactly 45. `backward_experts`: same law as forward_experts, drawn independently.
All inputs are finite; a program needn't handle non-finite values.
Results may differ from a plain program's by a relative error of at most 0.0054.
Values may be sent and summed in bfloat16 or wider, within the bound.
A program may use at most 128 MiB of HBM per device.

v0:
```python
import jax
import jax.numpy as jnp
from jax import lax
from jax.sharding import PartitionSpec as P

EPSILON = 1e-06


def passed_along(value, axis, steps):
    count = lax.axis_size(axis)
    initial, last = (max(0, -steps), min(count, count - steps))
    return lax.ppermute(value, axis, [(source, source + steps) for source in range(initial, last)])


def norm_scale(values, gain_row):
    widened = values.astype(jnp.float32)
    inverse = lax.rsqrt(jnp.mean(widened * widened, axis=-1, keepdims=True) + EPSILON)
    return widened * inverse * gain_row


def dense_weights(expert_ids, gates, expert_count):
    weights = gates / jnp.sum(gates, axis=-1, keepdims=True)
    onehot = expert_ids[:, :, None] == jnp.arange(expert_count, dtype=jnp.int32)[None, None, :]
    return jnp.sum(jnp.where(onehot, weights[:, :, None], 0.0), axis=1)


def local(
    forward_input,
    backward_cotangent,
    saved_input,
    saved_hidden,
    norm_gain,
    forward_experts,
    forward_gates,
    backward_experts,
    backward_gates,
    gate_up_weight,
    down_weight,
):
    peer_count = lax.axis_size("expert")
    me = lax.axis_index("expert")
    table = jnp.concatenate(
        [
            dense_weights(forward_experts[0], forward_gates[0], peer_count),
            dense_weights(backward_experts[0], backward_gates[0], peer_count),
        ],
        axis=1,
    )
    tables = lax.all_gather(table, "expert", axis=0, tiled=True)
    weight_f = lax.dynamic_slice_in_dim(tables, me, 1, axis=1)
    weight_b = lax.dynamic_slice_in_dim(tables, peer_count + me, 1, axis=1)
    moved_input, moved_cotangent = passed_along((forward_input, backward_cotangent), "section", 1)
    is_first = lax.axis_index("section") == 0
    layer_in = jnp.where(is_first, forward_input, moved_input)[0]
    cotangent = jnp.where(is_first, backward_cotangent, moved_cotangent)[0]
    token_count = layer_in.shape[0]
    slot_total = saved_hidden.shape[2]
    capacity = slot_total // peer_count
    gain_row = norm_gain[0]
    weight_in = gate_up_weight[0, 0]
    weight_down = down_weight[0, 0]
    hidden_width = weight_down.shape[0]
    normed = norm_scale(layer_in, gain_row).astype(jnp.bfloat16)
    all_normed = lax.all_gather(normed, "expert", axis=0, tiled=True)
    all_cotangent = lax.all_gather(cotangent, "expert", axis=0, tiled=True)
    projected = jnp.dot(all_normed, weight_in, preferred_element_type=jnp.float32)
    hidden = (jax.nn.silu(projected[:, :hidden_width]) * projected[:, hidden_width:]).astype(
        jnp.bfloat16
    )
    served = jnp.dot(hidden, weight_down, preferred_element_type=jnp.float32)
    served = (served * weight_f).astype(jnp.bfloat16)
    mixture = lax.psum_scatter(served, "expert", scatter_dimension=0, tiled=True)
    forward_output = (layer_in.astype(jnp.float32) + mixture.astype(jnp.float32)).astype(
        jnp.bfloat16
    )
    routed = (weight_b > 0.0).reshape(peer_count, token_count)
    slot = jnp.cumsum(routed.astype(jnp.int32), axis=1) - 1
    spread = (
        (slot[:, :, None] == jnp.arange(capacity, dtype=jnp.int32)[None, None, :])
        & routed[:, :, None]
    ).astype(jnp.bfloat16)
    saved = jnp.einsum(
        "jts,jsf->jtf",
        spread,
        saved_hidden[0, 0].reshape(peer_count, capacity, -1),
        preferred_element_type=jnp.float32,
    ).reshape(peer_count * token_count, -1)
    scaled = (weight_b * all_cotangent.astype(jnp.float32)).astype(jnp.bfloat16)
    grad_hidden = lax.dot_general(
        scaled, weight_down, (((1,), (1,)), ((), ())), preferred_element_type=jnp.float32
    )
    gate, up = (saved[:, :hidden_width], saved[:, hidden_width:])
    sig = jax.nn.sigmoid(gate)
    grad_both = jnp.concatenate(
        [grad_hidden * up * sig * (1.0 + gate * (1.0 - sig)), grad_hidden * gate * sig], axis=1
    ).astype(jnp.bfloat16)
    grads = lax.dot_general(
        grad_both, weight_in, (((1,), (1,)), ((), ())), preferred_element_type=jnp.float32
    ).astype(jnp.bfloat16)
    grad_normed = lax.psum_scatter(grads, "expert", scatter_dimension=0, tiled=True).astype(
        jnp.float32
    )

    def apply_norm(inputs):
        return norm_scale(inputs, gain_row)

    primal, pullback = jax.vjp(apply_norm, saved_input[0].astype(jnp.float32))
    input_gradient = (cotangent.astype(jnp.float32) + pullback(grad_normed)[0]).astype(jnp.bfloat16)
    return (forward_output[None], input_gradient[None])


def solution(mesh):
    row = P("section", "expert", None)
    block = P("section", "expert", None, None)
    in_specs = (row, row, row, block, P("section", None), row, row, row, row, block, block)
    return jax.shard_map(local, mesh=mesh, in_specs=in_specs, out_specs=(row, row), check_vma=False)
```

profile of v0, /device:TPU:0, one launch (start us, length us, event | category | flops | bytes accessed | tf_op | source)
XLA Modules:
  0.0 298.4 jit_solution(10791374151857974960)
XLA Ops:
  7.2 0.0 all-gather.7.cloned.1.call-start
  7.3 5.0 %collective-permute-start.1 = (bf16[1,72,4096]{2,1,0:T(8,128)(2,1)}, bf16[1,72,4096]{2,1,0:T(8,128)(2,1)S(1)}, u32[]{:S(2)}, u32[]{:S(2)}) collective-permute-start(bf16[1,72,4096]{2,1,0:T(8,128)(2,1)} %param.12), channel_id=1, source_target_pairs={{0,8},{8,16},{16,24},{1,9},{9,17},{17,25},{2,10},{10,18},{18,26},{... | collective-permute-start | bytes 1769480 | tf_op jit(solution)/shard_map/ppermute | solution.py:12
  12.3 12.8 %collective-permute-done.1 = bf16[1,72,4096]{2,1,0:T(8,128)(2,1)S(1)} collective-permute-done((bf16[1,72,4096]{2,1,0:T(8,128)(2,1)}, bf16[1,72,4096]{2,1,0:T(8,128)(2,1)S(1)}, u32[]{:S(2)}, u32[]{:S(2)}) %collective-permute-start.1) | collective-permute-done | bytes 589856 | tf_op jit(solution)/shard_map/ppermute | solution.py:12
  25.1 2.0 broadcast_select_fusion
  27.1 0.0 all-gather.7.cloned.1.call-update
  27.1 0.0 reduce-scatter.5.cloned.1.call-start
  27.3 14.3 %all-gather.1 = f32[8,72,16]{1,2,0:T(8,128)S(1)} all-gather(f32[1,72,16]{1,2,0:T(8,128)S(1)} %maximum_bitcast_fusion), channel_id=1, replica_groups=mesh['section'=4,'expert'=8] {'expert'}, dimensions={0}, use_global_device_ids=true | all-gather | bytes 41472 | tf_op jit(solution)/shard_map/all_gather | solution.py:49
  41.6 0.1 reshape.100
  41.7 0.3 reshape_squeeze.3
  42.1 0.1 reshape.92
  42.2 0.2 reduce_window_sum.11
  42.5 2.4 fusion.34
  44.9 35.2 %all-gather.7.cloned.1.call-done = bf16[1,576,4096]{2,1,0:T(8,128)(2,1)} async-done(((bf16[1,72,4096]{2,1,0:T(8,128)(2,1)}), bf16[1,576,4096]{2,1,0:T(8,128)(2,1)}) %all-gather.7.cloned.1.call-update) | async-done | bytes 4718608 | tf_op jit(solution)/shard_map/all_gather | solution.py:65
  80.1 9.4 %fusion.16 = (bf16[576,768]{1,0:T(8,128)(2,1)S(1)}, bf16[576,768]{1,0:T(8,128)(2,1)S(1)}) fusion(f32[576,1536]{1,0:T(8,128)} %bitcast.55, bf16[1,1,768,4096]{3,2,1,0:T(8,128)(2,1)} %param.21, bf16[1,576,4096]{2,1,0:T(8,128)(2,1)} %all-gather.7.cloned.1.call-done, f32[576]{0:T(1024)S(1)} %get-tuple-element.4), kind=kOutput, calls=%fused_computation.16 | convolution fusion | flops 3636707328 | bytes 16320768 | tf_op jit(solution)/shard_map/dot_general | solution.py:89
  89.6 18.4 %fusion.8 = bf16[576,4096]{1,0:T(8,128)(2,1)} fusion(bf16[1,1,4096,1536]{3,2,1,0:T(8,128)(2,1)} %param.20, bf16[576,768]{1,0:T(8,128)(2,1)S(1)} %get-tuple-element.9, bf16[576,768]{1,0:T(8,128)(2,1)S(1)} %get-tuple-element.8), kind=kOutput, calls=%fused_computation.10 | convolution fusion | flops 7253655552 | bytes 19070976 | tf_op jit(solution)/shard_map/dot_general | solution.py:97
  107.9 0.0 reduce-scatter.5.cloned.1.call-update
  108.0 0.0 all-gather.5.cloned.1.call-start
  108.0 1.0 copy-done.3
  109.0 3.4 %collective-permute-start = (bf16[1,72,4096]{2,1,0:T(8,128)(2,1)S(1)}, bf16[1,72,4096]{2,1,0:T(8,128)(2,1)S(1)}, u32[]{:S(2)}, u32[]{:S(2)}) collective-permute-start(bf16[1,72,4096]{2,1,0:T(8,128)(2,1)S(1)} %copy-done.3), channel_id=1, source_target_pairs={{0,8},{8,16},{16,24},{1,9},{9,17},{17,25},{2,10},{10,18},{18,26},{... | collective-permute-start | bytes 1769480 | tf_op jit(solution)/shard_map/ppermute | solution.py:12
  112.4 12.9 %collective-permute-done = bf16[1,72,4096]{2,1,0:T(8,128)(2,1)S(1)} collective-permute-done((bf16[1,72,4096]{2,1,0:T(8,128)(2,1)S(1)}, bf16[1,72,4096]{2,1,0:T(8,128)(2,1)S(1)}, u32[]{:S(2)}, u32[]{:S(2)}) %collective-permute-start) | collective-permute-done | bytes 589856 | tf_op jit(solution)/shard_map/ppermute | solution.py:12
  125.3 0.3 fusion.23
  125.6 36.1 %reduce-scatter.5.cloned.1.call-done = bf16[72,4096]{1,0:T(8,128)(2,1)} async-done(((bf16[576,4096]{1,0:T(8,128)(2,1)}), bf16[72,4096]{1,0:T(8,128)(2,1)}) %reduce-scatter.5.cloned.1.call-update) | async-done | bytes 589840 | tf_op jit(solution)/shard_map/reduce_scatter | solution.py:100
  161.7 1.4 fusion.27
  163.2 2.6 fusion.32
  165.9 0.0 all-gather.5.cloned.1.call-update
  165.9 0.2 reduce-scatter.3.cloned.1.call-start
  166.1 50.0 %all-gather.5.cloned.1.call-done = bf16[576,4096]{1,0:T(8,128)(2,1)} async-done(((bf16[72,4096]{1,0:T(8,128)(2,1)}), bf16[576,4096]{1,0:T(8,128)(2,1)}) %all-gather.5.cloned.1.call-update) | async-done | bytes 4718608 | tf_op jit(solution)/shard_map/all_gather | solution.py:64
  216.1 11.5 %fusion.2 = f32[576,1536]{1,0:T(8,128)S(1)} fusion(bf16[576,4096]{1,0:T(8,128)(2,1)} %all-gather.5.cloned.1.call-done, bf16[1,1,4096,1536]{3,2,1,0:T(8,128)(2,1)} %param.20), kind=kOutput, calls=%fused_computation.2 | convolution fusion | flops 7247757312 | bytes 20840448 | tf_op jit(solution)/shard_map/dot_general | solution.py:66
  227.5 8.4 %multiply_convert_fusion = bf16[576,4096]{1,0:T(8,128)(2,1)} fusion(bf16[1,1,768,4096]{3,2,1,0:T(8,128)(2,1)} %param.21, f32[576]{0:T(1024)S(1)} %get-tuple-element.5, f32[576,1536]{1,0:T(8,128)S(1)} %fusion.2), kind=kOutput, calls=%fused_computation.6 | convolution fusion | flops 3631251456 | bytes 14551296 | tf_op jit(solution)/shard_map/dot_general | solution.py:70
  235.9 0.0 reduce-scatter.3.cloned.1.call-update
  235.9 53.9 %reduce-scatter.3.cloned.1.call-done = bf16[72,4096]{1,0:T(8,128)(2,1)} async-done(((bf16[576,4096]{1,0:T(8,128)(2,1)}), bf16[72,4096]{1,0:T(8,128)(2,1)}) %reduce-scatter.3.cloned.1.call-update) | async-done | bytes 589840 | tf_op jit(solution)/shard_map/reduce_scatter | solution.py:72
  289.9 2.0 fusion.31
  (30 shorter events, 0.2 us)
Async XLA Ops:
  7.2 20.0 %copy-start.5 = (f32[1,72,4]{1,2,0:T(4,128)S(1)}, f32[1,72,4]{1,2,0:T(4,128)}, u32[]{:S(2)}) copy-start(f32[1,72,4]{1,2,0:T(4,128)} %param.19) | copy-start | bytes 3460
  7.2 20.0 %copy-start.6 = (f32[1,72,4]{1,2,0:T(4,128)S(1)}, f32[1,72,4]{1,2,0:T(4,128)}, u32[]{:S(2)}) copy-start(f32[1,72,4]{1,2,0:T(4,128)} %param.17) | copy-start | bytes 3460
  7.2 20.1 %copy-start.7 = (s32[1,72,4]{1,2,0:T(4,128)S(1)}, s32[1,72,4]{1,2,0:T(4,128)}, u32[]{:S(2)}) copy-start(s32[1,72,4]{1,2,0:T(4,128)} %param.18) | copy-start | bytes 3460
  7.2 20.1 %copy-start.8 = (s32[1,72,4]{1,2,0:T(4,128)S(1)}, s32[1,72,4]{1,2,0:T(4,128)}, u32[]{:S(2)}) copy-start(s32[1,72,4]{1,2,0:T(4,128)} %param.16) | copy-start | bytes 3460
  7.2 34.5 %copy-start.2 = (bf16[1,1,360,1536]{3,2,1,0:T(8,128)(2,1)S(1)}, bf16[1,1,360,1536]{3,2,1,0:T(8,128)(2,1)}, u32[]{:S(2)}) copy-start(bf16[1,1,360,1536]{3,2,1,0:T(8,128)(2,1)} %param.14) | copy-start | bytes 3317764
  7.2 72.9 %all-gather.7.cloned.1.call-start = ((), (), s32[]{:S(2)}) async-start(), calls=%async_computation.5 | async-start | bytes 5308416 | tf_op jit(solution)/shard_map/all_gather | solution.py:65
  7.3 17.9 %collective-permute-start.1 = (bf16[1,72,4096]{2,1,0:T(8,128)(2,1)}, bf16[1,72,4096]{2,1,0:T(8,128)(2,1)S(1)}, u32[]{:S(2)}, u32[]{:S(2)}) collective-permute-start(bf16[1,72,4096]{2,1,0:T(8,128)(2,1)} %param.12), channel_id=1, source_target_pairs={{0,8},{8,16},{16,24},{1,9},{9,17},{17,25},{2,10},{10,18},{18,26},{... | collective-permute-start | bytes 1769480 | tf_op jit(solution)/shard_map/ppermute | solution.py:12
  27.1 134.6 %reduce-scatter.5.cloned.1.call-start = ((), (), s32[]{:S(2)}) async-start(), calls=%async_computation.4 | async-start | bytes 5308416 | tf_op jit(solution)/shard_map/reduce_scatter | solution.py:100
  107.9 1.1 copy-start.3
  107.9 53.8 %copy-start.1 = (bf16[1,72,4096]{2,1,0:T(8,128)(2,1)S(1)}, bf16[1,72,4096]{2,1,0:T(8,128)(2,1)}, u32[]{:S(2)}) copy-start(bf16[1,72,4096]{2,1,0:T(8,128)(2,1)} %param.13) | copy-start | bytes 1769476
  107.9 53.8 %copy-start.4 = (f32[1,4096]{1,0:T(1,128)S(1)}, f32[1,4096]{1,0:T(1,128)}, u32[]{:S(2)}) copy-start(f32[1,4096]{1,0:T(1,128)} %param.15) | copy-start | bytes 49156
  108.0 55.2 %copy-start = (bf16[1,72,4096]{2,1,0:T(8,128)(2,1)S(1)}, bf16[1,72,4096]{2,1,0:T(8,128)(2,1)}, u32[]{:S(2)}) copy-start(bf16[1,72,4096]{2,1,0:T(8,128)(2,1)} %broadcast_select_fusion) | copy-start | bytes 1769476
  108.0 108.1 %all-gather.5.cloned.1.call-start = ((), (), s32[]{:S(2)}) async-start(), calls=%async_computation.2 | async-start | bytes 5308416 | tf_op jit(solution)/shard_map/all_gather | solution.py:64
  109.0 16.3 %collective-permute-start = (bf16[1,72,4096]{2,1,0:T(8,128)(2,1)S(1)}, bf16[1,72,4096]{2,1,0:T(8,128)(2,1)S(1)}, u32[]{:S(2)}, u32[]{:S(2)}) collective-permute-start(bf16[1,72,4096]{2,1,0:T(8,128)(2,1)S(1)} %copy-done.3), channel_id=1, source_target_pairs={{0,8},{8,16},{16,24},{1,9},{9,17},{17,25},{2,10},{10,18},{18,26},{... | collective-permute-start | bytes 1769480 | tf_op jit(solution)/shard_map/ppermute | solution.py:12
  165.9 124.0 %reduce-scatter.3.cloned.1.call-start = ((), (), s32[]{:S(2)}) async-start(), calls=%async_computation.3 | async-start | bytes 5308416 | tf_op jit(solution)/shard_map/reduce_scatter | solution.py:72
Sparse Core Ops, SparseCore 0:
  27.2 52.8 all-gather.6
  108.1 53.6 reduce-scatter.4
  166.0 50.0 all-gather.4
  236.1 53.7 reduce-scatter.2
where the time goes:
time: 299 us; the launch traced here: 298 us
  waiting for transfers between devices  201 us (67%)
  matrix products  50 us (17%)
  blocking collectives  14.3 us (5%)
  between operations  14 us (5%)
  starting transfers between devices  8.75 us (3%)
  other arithmetic  8.72 us (3%)
    reduce_scatter x1, waiting for transfers between devices, local(): lax.psum_scatter(served, 'expert', scatter_dimension=0, tiled=True)  53.9 us
    all_gather x1, waiting for transfers between devices, local(): all_normed = lax.all_gather(normed, 'expert', axis=0, tiled=True)  50 us
    reduce_scatter x1, waiting for transfers between devices, local(): lax.psum_scatter(grads, 'expert', scatter_dimension=0, tiled=True)  36.1 us
    all_gather x1, waiting for transfers between devices, local(): all_cotangent = lax.all_gather(cotangent, 'expert', axis=0, tiled=True)  35.2 us
    ppermute x2, waiting for transfers between devices, passed_along(): lax.ppermute(value, axis, [(source, source + steps) for source in range(i...  25.8 us
    dot_general x1, matrix products, local(): lax.dot_general(grad_both, weight_in, (((1,), (1,)), ((), ())), preferred...  18.4 us
    all_gather x1, blocking collectives, local(): tables = lax.all_gather(table, 'expert', axis=0, tiled=True)  14.3 us
    dot_general x1, matrix products, local(): jnp.dot(all_normed, weight_in, preferred_element_type=jnp.float32)  11.5 us
  transfers between devices with their start and end apart: 6, of which 6 were waited for; matrix products, arithmetic and copies ran while one was open for 1% of the time, Pallas kernels for 0%

commit v1 on v0

--- a/solution.py
+++ b/solution.py
@@ -61,7 +61,22 @@
     weight_down = down_weight[0, 0]
     hidden_width = weight_down.shape[0]
     normed = norm_scale(layer_in, gain_row).astype(jnp.bfloat16)
-    all_normed = lax.all_gather(normed, "expert", axis=0, tiled=True)
+    v_next, inter, heard = (lax.axis_size("expert"), lax.axis_index("expert"), normed.shape[0])
+    pages = [u * v_next if t == 0 else u for t, u in enumerate(normed.shape)]
+    b_now = w_next = normed
+    all_normed = lax.dynamic_update_slice_in_dim(
+        jnp.zeros(pages, normed.dtype), normed, inter * heard, axis=0
+    )
+    for j in tuple(range(1, v_next // 2 + 1)):
+        b_now = lax.ppermute(b_now, "expert", [(t, (t + 1) % v_next) for t in range(v_next)])
+        all_normed = lax.dynamic_update_slice_in_dim(
+            all_normed, b_now, (inter - j) % v_next * heard, axis=0
+        )
+        if 2 * j < v_next:
+            w_next = lax.ppermute(w_next, "expert", [(t, (t - 1) % v_next) for t in range(v_next)])
+            all_normed = lax.dynamic_update_slice_in_dim(
+                all_normed, w_next, (inter + j) % v_next * heard, axis=0
+            )
     all_cotangent = lax.all_gather(cotangent, "expert", axis=0, tiled=True)
     projected = jnp.dot(all_normed, weight_in, preferred_element_type=jnp.float32)
     hidden = (jax.nn.silu(projected[:, :hidden_width]) * projected[:, hidden_width:]).astype(

time: 299 us -> 277 us (0.926)
  waiting for transfers between devices: 201 us -> 125 us
  blocking collectives: 14.3 us -> 47.7 us
  starting transfers between devices: 8.75 us -> 19.3 us
  local copies, waits for them, and re-layouts: 1.55 us -> 10.5 us
  other arithmetic: 8.72 us -> 11.9 us
    all_gather x1 -> x0, waiting for transfers between devices: 50 us -> none  [local(): all_normed = lax.all_gather(normed, 'expert', axis=0, tiled=True)]
    all_gather x1, waiting for transfers between devices: 35.2 us -> 0.01 us  [local(): all_cotangent = lax.all_gather(cotangent, 'expert', axis=0, tiled=True)]
    all_gather x1, blocking collectives: 14.3 us -> 47.7 us  [local(): tables = lax.all_gather(table, 'expert', axis=0, tiled=True)]
    reduce_scatter x1, waiting for transfers between devices: 53.9 us -> 20.9 us  [local(): lax.psum_scatter(served, 'expert', scatter_dimension=0, tiled=True)]
    ppermute x0 -> x7, waiting for transfers between devices: none -> 32.1 us  [the longest x4 32.1 us: local(): lax.ppermute(b_now, 'expert', [(t, (t + 1) % v_next) for t in range(v_nex...]
    reduce_scatter x1, waiting for transfers between devices: 36.1 us -> 53.6 us  [local(): lax.psum_scatter(grads, 'expert', scatter_dimension=0, tiled=True)]
    ppermute x0 -> x7, starting transfers between devices: none -> 10.7 us  [the longest x3 10.3 us: local(): lax.ppermute(w_next, 'expert', [(t, (t - 1) % v_next) for t in range(v_ne...]
    ppermute x2, waiting for transfers between devices: 25.8 us -> 18.5 us  [passed_along(): lax.ppermute(value, axis, [(source, source + steps) for source in range(i...]
  transfers between devices with their start and end apart: 6 -> 12, of which waited for: 6 -> 7; matrix products, arithmetic and copies ran while one was open for 1% -> 24% of each run, Pallas kernels for 0% -> 0%
where the time goes in v1:
time: 277 us
  waiting for transfers between devices  125 us (45%)
  matrix products  48 us (17%)
  blocking collectives  47.7 us (17%)
  starting transfers between devices  19.3 us (7%)
  between operations  14.1 us (5%)
  other arithmetic  11.9 us (4%)
  local copies, waits for them, and re-layouts  10.5 us (4%)
    reduce_scatter x1, waiting for transfers between devices, local(): lax.psum_scatter(grads, 'expert', scatter_dimension=0, tiled=True)  53.6 us
    all_gather x1, blocking collectives, local(): tables = lax.all_gather(table, 'expert', axis=0, tiled=True)  47.7 us
    ppermute x4, waiting for transfers between devices, local(): lax.ppermute(b_now, 'expert', [(t, (t + 1) % v_next) for t in range(v_nex...  32.1 us
    reduce_scatter x1, waiting for transfers between devices, local(): lax.psum_scatter(served, 'expert', scatter_dimension=0, tiled=True)  20.9 us
    ppermute x2, waiting for transfers between devices, passed_along(): lax.ppermute(value, axis, [(source, source + steps) for source in range(i...  18.5 us
    dot_general x1, matrix products, local(): lax.dot_general(grad_both, weight_in, (((1,), (1,)), ((), ())), preferred...  18.5 us
    dot_general x1, matrix products, local(): jnp.dot(all_normed, weight_in, preferred_element_type=jnp.float32)  12.1 us
    ppermute x3, starting transfers between devices, local(): lax.ppermute(w_next, 'expert', [(t, (t - 1) % v_next) for t in range(v_ne...  10.3 us
  transfers between devices with their start and end apart: 12, of which 7 were waited for; matrix products, arithmetic and copies ran while one was open for 24% of the time, Pallas kernels for 0%

profile of v1, /device:TPU:0, one launch (start us, length us, event | category | flops | bytes accessed | tf_op | source)
XLA Modules:
  0.0 276.7 jit_solution(12103862402360429610)
XLA Ops:
  7.2 4.9 %collective-permute-start.8 = (bf16[1,72,4096]{2,1,0:T(8,128)(2,1)}, bf16[1,72,4096]{2,1,0:T(8,128)(2,1)S(1)}, u32[]{:S(2)}, u32[]{:S(2)}) collective-permute-start(bf16[1,72,4096]{2,1,0:T(8,128)(2,1)} %param.12), channel_id=1, source_target_pairs={{0,8},{8,16},{16,24},{1,9},{9,17},{17,25},{2,10},{10,18},{18,26},{... | collective-permute-start | bytes 1769480 | tf_op jit(solution)/shard_map/ppermute | solution.py:12
  12.1 3.4 %collective-permute-start = (bf16[1,72,4096]{2,1,0:T(8,128)(2,1)}, bf16[1,72,4096]{2,1,0:T(8,128)(2,1)S(1)}, u32[]{:S(2)}, u32[]{:S(2)}) collective-permute-start(bf16[1,72,4096]{2,1,0:T(8,128)(2,1)} %param.11), channel_id=1, source_target_pairs={{0,8},{8,16},{16,24},{1,9},{9,17},{17,25},{2,10},{10,18},{18,26},{... | collective-permute-start | bytes 1769480 | tf_op jit(solution)/shard_map/ppermute | solution.py:12
  15.5 10.6 %collective-permute-done.8 = bf16[1,72,4096]{2,1,0:T(8,128)(2,1)S(1)} collective-permute-done((bf16[1,72,4096]{2,1,0:T(8,128)(2,1)}, bf16[1,72,4096]{2,1,0:T(8,128)(2,1)S(1)}, u32[]{:S(2)}, u32[]{:S(2)}) %collective-permute-start.8) | collective-permute-done | bytes 589856 | tf_op jit(solution)/shard_map/ppermute | solution.py:12
  26.1 1.9 broadcast_select_fusion
  29.6 7.9 %collective-permute-done = bf16[1,72,4096]{2,1,0:T(8,128)(2,1)S(1)} collective-permute-done((bf16[1,72,4096]{2,1,0:T(8,128)(2,1)}, bf16[1,72,4096]{2,1,0:T(8,128)(2,1)S(1)}, u32[]{:S(2)}, u32[]{:S(2)}) %collective-permute-start) | collective-permute-done | bytes 589856 | tf_op jit(solution)/shard_map/ppermute | solution.py:12
  37.6 1.4 fusion.23
  39.1 2.7 broadcast_in_dim.40
  41.8 1.1 constant_dynamic-update-slice_fusion.7
  42.9 3.5 %collective-permute-start.2 = (bf16[72,4096]{1,0:T(8,128)(2,1)S(1)}, bf16[72,4096]{1,0:T(8,128)(2,1)S(1)}, u32[]{:S(2)}, u32[]{:S(2)}) collective-permute-start(bf16[72,4096]{1,0:T(8,128)(2,1)S(1)} %get-tuple-element.7), channel_id=1, source_target_pairs={{0,7},{1,0},{2,1},{3,2},{4,3},{5,4},{6,5},{7,6},{8,15},{9,8},{10,9... | collective-permute-start | bytes 1769480 | tf_op jit(solution)/shard_map/ppermute | solution.py:76
  46.5 47.7 %all-gather.1 = f32[8,72,16]{1,2,0:T(8,128)S(1)} all-gather(f32[1,72,16]{1,2,0:T(8,128)S(1)} %maximum_bitcast_fusion), channel_id=1, replica_groups=mesh['section'=4,'expert'=8] {'expert'}, dimensions={0}, use_global_device_ids=true | all-gather | bytes 41472 | tf_op jit(solution)/shard_map/all_gather | solution.py:49
  94.8 3.2 %collective-permute-start.4 = (bf16[72,4096]{1,0:T(8,128)(2,1)S(1)}, bf16[72,4096]{1,0:T(8,128)(2,1)S(1)}, u32[]{:S(2)}, u32[]{:S(2)}) collective-permute-start(bf16[72,4096]{1,0:T(8,128)(2,1)S(1)} %collective-permute-done.2), channel_id=1, source_target_pairs={{0,7},{1,0},{2,1},{3,2},{4,3},{5,4},{6,5},{7,6},{8,15},{9,8},{10,9... | collective-permute-start | bytes 1769480 | tf_op jit(solution)/shard_map/ppermute | solution.py:76
  98.0 0.9 constant_dynamic-update-slice_fusion.6
  99.0 0.9 constant_dynamic-update-slice_fusion.5
  99.8 11.8 %collective-permute-done.3 = bf16[72,4096]{1,0:T(8,128)(2,1)S(1)} collective-permute-done((bf16[72,4096]{1,0:T(8,128)(2,1)S(1)}, bf16[72,4096]{1,0:T(8,128)(2,1)S(1)}, u32[]{:S(2)}, u32[]{:S(2)}) %collective-permute-start.3) | collective-permute-done | bytes 589856 | tf_op jit(solution)/shard_map/ppermute | solution.py:71
  111.7 3.5 %collective-permute-start.6 = (bf16[72,4096]{1,0:T(8,128)(2,1)S(1)}, bf16[72,4096]{1,0:T(8,128)(2,1)S(1)}, u32[]{:S(2)}, u32[]{:S(2)}) collective-permute-start(bf16[72,4096]{1,0:T(8,128)(2,1)S(1)} %collective-permute-done.4), channel_id=1, source_target_pairs={{0,7},{1,0},{2,1},{3,2},{4,3},{5,4},{6,5},{7,6},{8,15},{9,8},{10,9... | collective-permute-start | bytes 1769480 | tf_op jit(solution)/shard_map/ppermute | solution.py:76
  115.2 0.9 constant_dynamic-update-slice_fusion.4
  117.0 10.8 %collective-permute-done.5 = bf16[72,4096]{1,0:T(8,128)(2,1)S(1)} collective-permute-done((bf16[72,4096]{1,0:T(8,128)(2,1)S(1)}, bf16[72,4096]{1,0:T(8,128)(2,1)S(1)}, u32[]{:S(2)}, u32[]{:S(2)}) %collective-permute-start.5) | collective-permute-done | bytes 589856 | tf_op jit(solution)/shard_map/ppermute | solution.py:71
  127.8 0.9 constant_dynamic-update-slice_fusion.2
  128.7 0.9 constant_dynamic-update-slice_fusion.1
  129.6 9.4 %collective-permute-done.7 = bf16[72,4096]{1,0:T(8,128)(2,1)S(1)} collective-permute-done((bf16[72,4096]{1,0:T(8,128)(2,1)S(1)}, bf16[72,4096]{1,0:T(8,128)(2,1)S(1)}, u32[]{:S(2)}, u32[]{:S(2)}) %collective-permute-start.7) | collective-permute-done | bytes 589856 | tf_op jit(solution)/shard_map/ppermute | solution.py:71
  138.9 0.8 constant_dynamic-update-slice_fusion
  139.8 12.1 %fusion.2 = f32[576,1536]{1,0:T(8,128)S(1)} fusion(bf16[576,4096]{1,0:T(8,128)(2,1)} %constant_dynamic-update-slice_fusion, bf16[1,1,4096,1536]{3,2,1,0:T(8,128)(2,1)} %param.20), kind=kOutput, calls=%fused_computation.2 | convolution fusion | flops 7247757312 | bytes 20840448 | tf_op jit(solution)/shard_map/dot_general | solution.py:81
  151.9 5.6 %multiply_convert_fusion = bf16[576,4096]{1,0:T(8,128)(2,1)} fusion(bf16[1,1,768,4096]{3,2,1,0:T(8,128)(2,1)S(1)} %bitcast.63, f32[576]{0:T(1024)S(1)} %get-tuple-element.5, f32[576,1536]{1,0:T(8,128)S(1)} %fusion.2), kind=kOutput, calls=%fused_computation.6 | convolution fusion | flops 3631251456 | bytes 14551296 | tf_op jit(solution)/shard_map/dot_general | solution.py:85
  157.7 1.0 copy-done.2
  159.4 2.5 fusion.34
  161.9 9.4 %fusion.16 = (bf16[576,768]{1,0:T(8,128)(2,1)S(1)}, bf16[576,768]{1,0:T(8,128)(2,1)S(1)}) fusion(f32[576,1536]{1,0:T(8,128)} %bitcast.56, bf16[1,1,768,4096]{3,2,1,0:T(8,128)(2,1)} %param.21, bf16[1,576,4096]{2,1,0:T(8,128)(2,1)} %all-gather.4.cloned.1.call-done, f32[576]{0:T(1024)S(1)} %get-tuple-element.4), kind=kOutput, calls=%fused_computation.16 | convolution fusion | flops 3636707328 | bytes 16320768 | tf_op jit(solution)/shard_map/dot_general | solution.py:104
  171.3 18.5 %fusion.8 = bf16[576,4096]{1,0:T(8,128)(2,1)} fusion(bf16[1,1,4096,1536]{3,2,1,0:T(8,128)(2,1)} %param.20, bf16[576,768]{1,0:T(8,128)(2,1)S(1)} %get-tuple-element.11, bf16[576,768]{1,0:T(8,128)(2,1)S(1)} %get-tuple-element.10), kind=kOutput, calls=%fused_computation.10 | convolution fusion | flops 7253655552 | bytes 19070976 | tf_op jit(solution)/shard_map/dot_general | solution.py:112
  189.8 20.9 %reduce-scatter.3.cloned.1.call-done = bf16[72,4096]{1,0:T(8,128)(2,1)} async-done(((bf16[576,4096]{1,0:T(8,128)(2,1)}), bf16[72,4096]{1,0:T(8,128)(2,1)}) %reduce-scatter.3.cloned.1.call-update) | async-done | bytes 589840 | tf_op jit(solution)/shard_map/reduce_scatter | solution.py:87
  210.7 2.0 fusion.31
  212.7 53.6 %reduce-scatter.5.cloned.1.call-done = bf16[72,4096]{1,0:T(8,128)(2,1)} async-done(((bf16[576,4096]{1,0:T(8,128)(2,1)}), bf16[72,4096]{1,0:T(8,128)(2,1)}) %reduce-scatter.5.cloned.1.call-update) | async-done | bytes 589840 | tf_op jit(solution)/shard_map/reduce_scatter | solution.py:115
  266.4 1.4 fusion.27
  267.8 2.3 fusion.32
  (53 shorter events, 3.9 us)
Async XLA Ops:
  7.2 154.7 %all-gather.4.cloned.1.call-start = ((), (), s32[]{:S(2)}) async-start(), calls=%async_computation.4 | async-start | bytes 5308416 | tf_op jit(solution)/shard_map/all_gather | solution.py:80
  7.2 18.9 %collective-permute-start.8 = (bf16[1,72,4096]{2,1,0:T(8,128)(2,1)}, bf16[1,72,4096]{2,1,0:T(8,128)(2,1)S(1)}, u32[]{:S(2)}, u32[]{:S(2)}) collective-permute-start(bf16[1,72,4096]{2,1,0:T(8,128)(2,1)} %param.12), channel_id=1, source_target_pairs={{0,8},{8,16},{16,24},{1,9},{9,17},{17,25},{2,10},{10,18},{18,26},{... | collective-permute-start | bytes 1769480 | tf_op jit(solution)/shard_map/ppermute | solution.py:12
  12.1 25.5 %collective-permute-start = (bf16[1,72,4096]{2,1,0:T(8,128)(2,1)}, bf16[1,72,4096]{2,1,0:T(8,128)(2,1)S(1)}, u32[]{:S(2)}, u32[]{:S(2)}) collective-permute-start(bf16[1,72,4096]{2,1,0:T(8,128)(2,1)} %param.11), channel_id=1, source_target_pairs={{0,8},{8,16},{16,24},{1,9},{9,17},{17,25},{2,10},{10,18},{18,26},{... | collective-permute-start | bytes 1769480 | tf_op jit(solution)/shard_map/ppermute | solution.py:12
  28.0 13.8 %copy-start.3 = (f32[1,4096]{1,0:T(1,128)S(1)}, f32[1,4096]{1,0:T(1,128)}, u32[]{:S(2)}) copy-start(f32[1,4096]{1,0:T(1,128)} %param.15) | copy-start | bytes 49156
  28.1 182.7 %reduce-scatter.3.cloned.1.call-start = ((), (), s32[]{:S(2)}) async-start(), calls=%async_computation.2 | async-start | bytes 5308416 | tf_op jit(solution)/shard_map/reduce_scatter | solution.py:87
  39.0 7.4 %copy-start.4 = (f32[1,72,4]{1,2,0:T(4,128)S(1)}, f32[1,72,4]{1,2,0:T(4,128)}, u32[]{:S(2)}) copy-start(f32[1,72,4]{1,2,0:T(4,128)} %param.19) | copy-start | bytes 3460
  39.0 7.4 %copy-start.5 = (f32[1,72,4]{1,2,0:T(4,128)S(1)}, f32[1,72,4]{1,2,0:T(4,128)}, u32[]{:S(2)}) copy-start(f32[1,72,4]{1,2,0:T(4,128)} %param.17) | copy-start | bytes 3460
  39.0 7.4 %copy-start.6 = (s32[1,72,4]{1,2,0:T(4,128)S(1)}, s32[1,72,4]{1,2,0:T(4,128)}, u32[]{:S(2)}) copy-start(s32[1,72,4]{1,2,0:T(4,128)} %param.18) | copy-start | bytes 3460
  39.0 7.4 %copy-start.7 = (s32[1,72,4]{1,2,0:T(4,128)S(1)}, s32[1,72,4]{1,2,0:T(4,128)}, u32[]{:S(2)}) copy-start(s32[1,72,4]{1,2,0:T(4,128)} %param.16) | copy-start | bytes 3460
  42.9 51.5 %collective-permute-start.1 = (bf16[72,4096]{1,0:T(8,128)(2,1)S(1)}, bf16[72,4096]{1,0:T(8,128)(2,1)S(1)}, u32[]{:S(2)}, u32[]{:S(2)}) collective-permute-start(bf16[72,4096]{1,0:T(8,128)(2,1)S(1)} %get-tuple-element.7), channel_id=1, source_target_pairs={{0,1},{1,2},{2,3},{3,4},{4,5},{5,6},{6,7},{7,0},{8,9},{9,10},{10,1... | collective-permute-start | bytes 1769480 | tf_op jit(solution)/shard_map/ppermute | solution.py:71
  42.9 51.9 %collective-permute-start.2 = (bf16[72,4096]{1,0:T(8,128)(2,1)S(1)}, bf16[72,4096]{1,0:T(8,128)(2,1)S(1)}, u32[]{:S(2)}, u32[]{:S(2)}) collective-permute-start(bf16[72,4096]{1,0:T(8,128)(2,1)S(1)} %get-tuple-element.7), channel_id=1, source_target_pairs={{0,7},{1,0},{2,1},{3,2},{4,3},{5,4},{6,5},{7,6},{8,15},{9,8},{10,9... | collective-permute-start | bytes 1769480 | tf_op jit(solution)/shard_map/ppermute | solution.py:76
  94.4 17.2 %collective-permute-start.3 = (bf16[72,4096]{1,0:T(8,128)(2,1)S(1)}, bf16[72,4096]{1,0:T(8,128)(2,1)S(1)}, u32[]{:S(2)}, u32[]{:S(2)}) collective-permute-start(bf16[72,4096]{1,0:T(8,128)(2,1)S(1)} %collective-permute-done.1), channel_id=1, source_target_pairs={{0,1},{1,2},{2,3},{3,4},{4,5},{5,6},{6,7},{7,0},{8,9},{9,10},{10,1... | collective-permute-start | bytes 1769480 | tf_op jit(solution)/shard_map/ppermute | solution.py:71
  94.8 16.9 %collective-permute-start.4 = (bf16[72,4096]{1,0:T(8,128)(2,1)S(1)}, bf16[72,4096]{1,0:T(8,128)(2,1)S(1)}, u32[]{:S(2)}, u32[]{:S(2)}) collective-permute-start(bf16[72,4096]{1,0:T(8,128)(2,1)S(1)} %collective-permute-done.2), channel_id=1, source_target_pairs={{0,7},{1,0},{2,1},{3,2},{4,3},{5,4},{6,5},{7,6},{8,15},{9,8},{10,9... | collective-permute-start | bytes 1769480 | tf_op jit(solution)/shard_map/ppermute | solution.py:76
  111.7 16.2 %collective-permute-start.5 = (bf16[72,4096]{1,0:T(8,128)(2,1)S(1)}, bf16[72,4096]{1,0:T(8,128)(2,1)S(1)}, u32[]{:S(2)}, u32[]{:S(2)}) collective-permute-start(bf16[72,4096]{1,0:T(8,128)(2,1)S(1)} %collective-permute-done.3), channel_id=1, source_target_pairs={{0,1},{1,2},{2,3},{3,4},{4,5},{5,6},{6,7},{7,0},{8,9},{9,10},{10,1... | collective-permute-start | bytes 1769480 | tf_op jit(solution)/shard_map/ppermute | solution.py:71
  111.7 17.0 %collective-permute-start.6 = (bf16[72,4096]{1,0:T(8,128)(2,1)S(1)}, bf16[72,4096]{1,0:T(8,128)(2,1)S(1)}, u32[]{:S(2)}, u32[]{:S(2)}) collective-permute-start(bf16[72,4096]{1,0:T(8,128)(2,1)S(1)} %collective-permute-done.4), channel_id=1, source_target_pairs={{0,7},{1,0},{2,1},{3,2},{4,3},{5,4},{6,5},{7,6},{8,15},{9,8},{10,9... | collective-permute-start | bytes 1769480 | tf_op jit(solution)/shard_map/ppermute | solution.py:76
  127.8 11.1 %collective-permute-start.7 = (bf16[72,4096]{1,0:T(8,128)(2,1)S(1)}, bf16[72,4096]{1,0:T(8,128)(2,1)S(1)}, u32[]{:S(2)}, u32[]{:S(2)}) collective-permute-start(bf16[72,4096]{1,0:T(8,128)(2,1)S(1)} %collective-permute-done.5), channel_id=1, source_target_pairs={{0,1},{1,2},{2,3},{3,4},{4,5},{5,6},{6,7},{7,0},{8,9},{9,10},{10,1... | collective-permute-start | bytes 1769480 | tf_op jit(solution)/shard_map/ppermute | solution.py:71
  138.9 12.9 %slice-start = ((s8[6291456]{0:T(1024)(128)(4,1)}), s8[4194304]{0:T(1024)(128)(4,1)S(1)}, s32[]{:S(2)}) async-start(s8[6291456]{0:T(1024)(128)(4,1)} %bitcast.62), calls=%async_computation.5 | async-start | bytes 8388608
  139.8 12.1 %slice-start.1 = ((s8[6291456]{0:T(1024)(128)(4,1)}), s8[2097152]{0:T(1024)(128)(4,1)S(1)}, s32[]{:S(2)}) async-start(s8[6291456]{0:T(1024)(128)(4,1)} %bitcast.62), calls=%async_computation.6 | async-start | bytes 4194304
  157.5 1.2 copy-start.2
  157.5 108.9 %reduce-scatter.5.cloned.1.call-start = ((), (), s32[]{:S(2)}) async-start(), calls=%async_computation.3 | async-start | bytes 5308416 | tf_op jit(solution)/shard_map/reduce_scatter | solution.py:115
  189.8 76.6 %copy-start.1 = (bf16[1,72,4096]{2,1,0:T(8,128)(2,1)S(1)}, bf16[1,72,4096]{2,1,0:T(8,128)(2,1)}, u32[]{:S(2)}) copy-start(bf16[1,72,4096]{2,1,0:T(8,128)(2,1)} %param.13) | copy-start | bytes 1769476
  189.8 78.0 %copy-start = (bf16[1,72,4096]{2,1,0:T(8,128)(2,1)S(1)}, bf16[1,72,4096]{2,1,0:T(8,128)(2,1)}, u32[]{:S(2)}) copy-start(bf16[1,72,4096]{2,1,0:T(8,128)(2,1)} %broadcast_select_fusion) | copy-start | bytes 1769476
Sparse Core Ops, SparseCore 0:
  28.2 65.5 all-gather.3
  157.6 53.0 reduce-scatter.2
  213.0 53.3 reduce-scatter.4
